TPU v7x, 256 devices: a whole 4x4x8 slice. The times are simulated.
256 devices in a mesh: seq: 32 (over z, x), head: 8 (over y, core).
Axes of the slice: x: 4, y: 4, z: 8, core: 2. Of those that a mesh axis runs over, the one named last changes fastest.
Arguments:
- queries: bfloat16 [32768, 4096], P('seq', 'head'), may hold values from -6 to 6
- key_rows: bfloat16 [32768, 4096], P('seq', 'head'), may hold values from -6 to 6
- value_rows: bfloat16 [32768, 4096], P('seq', 'head'), may hold values from -6 to 6
- out_grad: bfloat16 [32768, 4096], P('seq', 'head'), may hold values from -6 to 6
- cache_states: bfloat16 [32, 32, 128, 128], P('seq', 'head'), may hold values from -96 to 96
- session_start: int32 [32], P('seq'), may hold values from 0 to 1024, as said below
- cache_owner: int32 [32], replicated, may hold values from 0 to 31, as said below
- probe_gate: float32 [32768], P('seq'), may hold values from 0.1 to 4.5
- steer_vector: bfloat16 [32, 128], P('head'), may hold values from -0.09375 to 0.09375
Outputs:
- grad_queries: bfloat16 [32768, 4096], P('seq', 'head')
- grad_keys: bfloat16 [32768, 4096], P('seq', 'head')
- grad_values: bfloat16 [32768, 4096], P('seq', 'head')
- grad_cache: bfloat16 [32, 32, 128, 128], P('seq', 'head')
- grad_steer: float32 [32, 128], P('head')
- grad_gate: float32 [32768], P('seq')
Inputs may be any that keep to these rules, and one draw needn't show every extreme that they name: session_start[b] is the position of the session beginning in block b, or 1024 where none does; it is 512 for every b with b % 4 == 3, so no session reaches across more than 5 blocks. `cache_owner`: a permutation of the slots.
All inputs are finite; a program needn't handle non-finite values.
Results may differ from a plain program's by a relative error of at most 0.007.
Values may be sent and summed in bfloat16 or wider, within the bound.
No kernel may reach another device: no remote copies, remote signals or barrier semaphores. Data moves between devices by JAX's collectives and lax.ppermute only.
A program may use at most 128 MiB of HBM per device.

v0:
```python
import math
import jax
import jax.numpy as jnp
from jax import lax
from jax.sharding import PartitionSpec as P

DK = 128
DV = 128


def prefix(part, axis, combine, identity, reverse):
    count = lax.axis_size(axis)
    place = lax.axis_index(axis)
    ahead = count - 1 - place if reverse else place
    gathered = jax.tree.map(lambda a: lax.all_gather(a, axis), part)
    state = jax.tree.map(lambda a, e: jnp.zeros_like(a) + jnp.asarray(e, a.dtype), part, identity)

    def one(turn, state):
        source = count - 1 - turn if reverse else turn
        return combine(
            state, jax.tree.map(lambda a: lax.dynamic_index_in_dim(a, source, 0, False), gathered)
        )

    return lax.fori_loop(0, ahead, one, state)


def pairwise_dot(left_rows, right_rows):
    return lax.dot_general(
        left_rows, right_rows, (((1,), (1,)), ((), ())), preferred_element_type=jnp.float32
    )


def leading_dot(left_rows, right_rows):
    return lax.dot_general(
        left_rows, right_rows, (((0,), (0,)), ((), ())), preferred_element_type=jnp.float32
    )


def combine_states(earlier_item, later_item):
    return (
        jnp.maximum(earlier_item[0], later_item[0]),
        jnp.where(later_item[0] > 0, later_item[1], earlier_item[1] + later_item[1]),
    )


def shards(
    queries,
    key_rows,
    value_rows,
    out_grad,
    cache_states,
    session_start,
    cache_owner,
    probe_gate,
    steer_vector,
):
    length = queries.shape[0]
    heads_here = steer_vector.shape[0]
    scaling = 1.0 / DK
    blocks_total = lax.axis_size("seq")
    block_index = lax.axis_index("seq")
    start_pos = session_start[0]
    reset_flag = (start_pos < length).astype(jnp.float32)
    positions = jnp.arange(length)
    before_start = positions < start_pos
    after_start = positions >= start_pos
    final_part = after_start | (start_pos >= length)
    causal = (positions[None, :] <= positions[:, None]) & (
        after_start[:, None] == after_start[None, :]
    )
    target = cache_owner[block_index]
    zero_state = jnp.zeros((heads_here, DK, DV), jnp.float32)
    shard_piece = lax.all_gather(cache_states, "seq", axis=0, tiled=True)
    slot_ids = jnp.arange(shard_piece.shape[0])
    weights = (slot_ids == target).astype(jnp.bfloat16)
    owned_state = lax.dot_general(
        weights, shard_piece, (((0,), (0,)), ((), ())), preferred_element_type=jnp.float32
    ).astype(jnp.bfloat16)
    query_heads = queries.reshape(length, heads_here, DK)
    key_heads = key_rows.reshape(length, heads_here, DK)
    value_heads = value_rows.reshape(length, heads_here, DV)
    grad_heads = out_grad.reshape(length, heads_here, DV)
    before_mask = before_start.astype(jnp.bfloat16)[:, None]
    after_mask = after_start.astype(jnp.bfloat16)[:, None]
    final_mask = final_part.astype(jnp.bfloat16)[:, None]
    kv_final = jnp.einsum(
        "thd,the->hde",
        key_heads * final_mask[:, :, None],
        value_heads,
        preferred_element_type=jnp.float32,
    )
    tail_state = jnp.where(reset_flag > 0, owned_state.astype(jnp.float32) + kv_final, kv_final)
    head_state = scaling * jnp.einsum(
        "thd,the->hde",
        query_heads * before_mask[:, :, None],
        grad_heads,
        preferred_element_type=jnp.float32,
    )
    start_state = scaling * jnp.einsum(
        "thd,the->hde",
        query_heads * after_mask[:, :, None],
        grad_heads,
        preferred_element_type=jnp.float32,
    )
    identity = (jnp.zeros((), jnp.float32), zero_state)
    entering = prefix((reset_flag, tail_state), "seq", combine_states, identity, False)[1]
    leaving = prefix((reset_flag, head_state), "seq", combine_states, identity, True)[1]
    start_grad = jnp.where(reset_flag > 0, start_state + leaving, 0.0).astype(jnp.bfloat16)
    slot_ids = jnp.arange(lax.axis_size("seq") * 1)
    weights = (slot_ids == target).astype(jnp.float32)
    grad_cache = lax.psum_scatter(
        (weights[:, None, None, None] * start_grad.astype(jnp.float32)[None]).astype(jnp.bfloat16),
        "seq",
        scatter_dimension=0,
        tiled=True,
    )
    entering_low = entering.astype(jnp.bfloat16)
    leaving_low = leaving.astype(jnp.bfloat16)
    query_grads = []
    key_grads = []
    value_grads = []
    for head_index in range(heads_here):
        query_head = queries[:, head_index * DK : (head_index + 1) * DK]
        key_head = key_rows[:, head_index * DK : (head_index + 1) * DK]
        value_head = value_rows[:, head_index * DV : (head_index + 1) * DV]
        grad_head = out_grad[:, head_index * DV : (head_index + 1) * DV]
        grad_scores = jnp.where(causal, scaling * pairwise_dot(grad_head, value_head), 0.0).astype(
            jnp.bfloat16
        )
        key_scores = jnp.where(causal, scaling * pairwise_dot(query_head, key_head), 0.0).astype(
            jnp.bfloat16
        )
        inter_query = pairwise_dot(grad_head * before_mask, entering_low[head_index])
        inter_query = inter_query + pairwise_dot(grad_head * after_mask, owned_state[head_index])
        grad_query = (
            jnp.dot(grad_scores, key_head, preferred_element_type=jnp.float32)
            + scaling * inter_query
        )
        grad_key = leading_dot(grad_scores, query_head) + pairwise_dot(
            value_head * final_mask, leaving_low[head_index]
        )
        grad_value = leading_dot(key_scores, grad_head) + jnp.dot(
            key_head * final_mask, leaving_low[head_index], preferred_element_type=jnp.float32
        )
        query_grads.append(grad_query.astype(jnp.bfloat16))
        key_grads.append(grad_key.astype(jnp.bfloat16))
        value_grads.append(grad_value.astype(jnp.bfloat16))
    grad_queries = jnp.concatenate(query_grads, axis=1)
    grad_keys = jnp.concatenate(key_grads, axis=1)
    grad_values = jnp.concatenate(value_grads, axis=1)
    steer_part = jnp.einsum("t,tc->c", probe_gate, out_grad, preferred_element_type=jnp.float32)
    grad_steer = lax.psum(steer_part, "seq").reshape(heads_here, DV) / math.sqrt(
        length * blocks_total
    )
    gate_part = jnp.dot(out_grad, steer_vector.reshape(-1), preferred_element_type=jnp.float32)
    grad_gate = lax.psum(gate_part, "head")
    return (grad_queries, grad_keys, grad_values, grad_cache, grad_steer, grad_gate)


def solution(mesh):
    in_specs = (
        P("seq", "head"),
        P("seq", "head"),
        P("seq", "head"),
        P("seq", "head"),
        P("seq", "head", None, None),
        P("seq"),
        P(),
        P("seq"),
        P("head", None),
    )
    out_specs = (
        P("seq", "head"),
        P("seq", "head"),
        P("seq", "head"),
        P("seq", "head", None, None),
        P("head", None),
        P("seq"),
    )
    return jax.shard_map(shards, mesh=mesh, in_specs=in_specs, out_specs=out_specs, check_vma=False)
```

profile of v0, /device:TPU:8, one launch (start us, length us, event | category | flops | bytes accessed | tf_op | source)
XLA Modules:
  0.0 521.7 jit_solution(7952977365945046856)
XLA Ops:
  10.1 2.8 convolution_multiply_fusion.1
  14.2 81.1 %all-gather.6.cloned.1.call-done = bf16[32,4,128,128]{3,2,1,0:T(8,128)(2,1)} async-done(((bf16[1,4,128,128]{3,2,1,0:T(8,128)(2,1)}), bf16[32,4,128,128]{3,2,1,0:T(8,128)(2,1)}) %all-gather.6.cloned.1.call-update) | async-done | bytes 4194320 | tf_op jit(solution)/shard_map/all_gather | solution.py:73
  95.3 5.4 %fusion = f32[1,4,128,128]{3,0,2,1:T(1,128)S(1)} fusion(bf16[32,4,128,128]{3,2,1,0:T(8,128)(2,1)} %all-gather.6.cloned.1.call-done, s32[]{:T(128)} %bitcast.7), kind=kOutput, calls=%fused_computation.3 | convolution fusion | flops 4194336 | bytes 4456452 | tf_op jit(solution)/shard_map/dot_general | solution.py:76
  103.7 73.2 %all-reduce.1 = (f32[32]{0:T(128)S(1)}, f32[512]{0:T(512)S(1)}) all-reduce(f32[32]{0:T(128)S(1)} %dynamic-update-slice, f32[512]{0:T(512)S(1)} %bitcast.121), channel_id=1, replica_groups=mesh['seq'=32,'head'=8] {'seq'}, use_global_device_ids=true, to_apply=%add | all-reduce | flops 544 | bytes 4352
  177.2 11.4 %psum.15 = f32[1024]{0:T(1024)} all-reduce(f32[1024]{0:T(1024)S(1)} %bitcast.120), channel_id=1, replica_groups=mesh['seq'=32,'head'=8] {'head'}, use_global_device_ids=true, to_apply=%region_6.7 | all-reduce | flops 1024 | bytes 8192 | tf_op jit(solution)/shard_map/psum | solution.py:156
  189.3 1.8 select_convert_fusion.4
  192.5 2.2 fusion.66
  202.5 72.2 %while.27 = (s32[]{:T(128)}, f32[4,128,128]{2,1,0:T(8,128)S(1)}, s32[]{:T(128)}, f32[32]{0:T(128)S(1)}, f32[32,4,128,128]{3,2,1,0:T(8,128)}, /*index=5*/s32[]{:T(128)}, s32[]{:T(128)}, s32[]{:T(128)}, s32[]{:T(128)}, f32[1]{0:T(128)}) while((s32[]{:T(128)}, f32[4,128,128]{2,1,0:T(8,128)S(1)}, s32[]{:T(128)}, f32[32]{0:T(128)S(1)}, ...), condition=%wide.region_3.4_spmd, body=%wide.region_2.3_spmd.sunk | while | flops 131079 | bytes 786613 | solution.py:24
  274.7 1.7 fusion.26
  276.4 3.1 multiply_convert_fusion
  280.1 2.3 fusion.70
  282.4 3.0 fusion.3
  285.5 3.0 fusion.4
  288.5 3.0 fusion.5
  291.5 3.0 fusion.6
  294.6 1.6 fusion.18
  296.2 1.5 fusion.17
  297.7 1.5 fusion.16
  299.3 1.5 fusion.15
  301.9 2.3 copy.32
  305.7 1.5 fusion.12
  308.7 1.5 fusion.13
  311.3 2.3 copy.31
  321.8 193.4 %reduce-scatter.2.cloned.1.call-done = bf16[1,4,128,128]{3,2,1,0:T(8,128)(2,1)} async-done(((bf16[32,4,128,128]{3,2,1,0:T(8,128)(2,1)}), bf16[1,4,128,128]{3,2,1,0:T(8,128)(2,1)}) %reduce-scatter.2.cloned.1.call-update) | async-done | bytes 131088 | tf_op jit(solution)/shard_map/reduce_scatter | solution.py:111
  (156 shorter events, 81.3 us)
Async XLA Ops:
  7.2 96.2 %copy-start = (f32[1024]{0:T(1024)S(1)}, f32[1024]{0:T(1024)}, u32[]{:S(2)}) copy-start(f32[1024]{0:T(1024)} %param.20) | copy-start | bytes 12292
  7.2 5.8 %copy-start.8 = (bf16[1024,512]{1,0:T(8,128)(2,1)S(1)}, bf16[1024,512]{1,0:T(8,128)(2,1)}, u32[]{:S(2)}) copy-start(bf16[1024,512]{1,0:T(8,128)(2,1)} %param.14) | copy-start | bytes 3145732
  7.2 6.4 %copy-start.17 = (s32[32]{0:T(128)S(1)}, s32[32]{0:T(128)}, u32[]{:S(2)}) copy-start(s32[32]{0:T(128)} %param.19) | copy-start | bytes 388
  7.2 88.1 %all-gather.6.cloned.1.call-start = ((), (), s32[]{:S(2)}) async-start(), calls=%async_computation.1 | async-start | bytes 4325376 | tf_op jit(solution)/shard_map/all_gather | solution.py:73
  7.9 194.6 %all-gather.10.cloned.1.call-start = ((), (), s32[]{:S(2)}) async-start(), calls=%async_computation.4 | async-start | bytes 8650752 | tf_op jit(solution)/shard_map/all_gather | solution.py:15
  10.1 85.2 %copy-start.11 = (bf16[1024,512]{0,1:T(8,128)(2,1)}, bf16[1024,512]{0,1:T(8,128)(2,1)S(1)}, u32[]{:S(2)}) copy-start(bf16[1024,512]{0,1:T(8,128)(2,1)S(1)} %copy.37) | copy-start | bytes 3145732
  12.9 300.6 %all-gather.8.cloned.1.call-start = ((), (), s32[]{:S(2)}) async-start(), calls=%async_computation.3 | async-start | bytes 8650752 | tf_op jit(solution)/shard_map/all_gather | solution.py:15
  95.3 5.5 %copy-start.12 = (bf16[1024,512]{1,0:T(8,128)(2,1)S(1)}, bf16[1024,512]{1,0:T(8,128)(2,1)}, u32[]{:S(2)}) copy-start(bf16[1024,512]{1,0:T(8,128)(2,1)} %param.15) | copy-start | bytes 3145732
  95.3 6.7 %copy-start.16 = (bf16[4,128]{1,0:T(4,128)(2,1)S(1)}, bf16[4,128]{1,0:T(4,128)(2,1)}, u32[]{:S(2)}) copy-start(bf16[4,128]{1,0:T(4,128)(2,1)} %param.21) | copy-start | bytes 3076
  95.3 6.7 %copy-start.19 = (u32[256]{0:T(256)S(1)}, u32[256]{0:T(256)}, u32[]{:S(2)}) copy-start(u32[256]{0:T(256)} %constant.87) | copy-start | bytes 3076
  95.3 8.1 %copy-start.1 = (bf16[1024,512]{1,0:T(8,128)(2,1)S(1)}, bf16[1024,512]{1,0:T(8,128)(2,1)}, u32[]{:S(2)}) copy-start(bf16[1024,512]{1,0:T(8,128)(2,1)} %param.16) | copy-start | bytes 3145732
  100.8 88.5 %copy-start.14 = (bf16[4,128,128]{2,1,0:T(8,128)(2,1)}, bf16[4,128,128]{2,1,0:T(8,128)(2,1)S(1)}, u32[]{:S(2)}) copy-start(bf16[4,128,128]{2,1,0:T(8,128)(2,1)S(1)} %convert_element_type.128) | copy-start | bytes 393220
  102.0 413.2 %reduce-scatter.2.cloned.1.call-start = ((), (), s32[]{:S(2)}) async-start(), calls=%async_computation.2 | async-start | bytes 4325376 | tf_op jit(solution)/shard_map/reduce_scatter | solution.py:111
  189.3 5.4 %copy-start.13 = (bf16[1024,512]{1,0:T(8,128)(2,1)S(1)}, bf16[1024,512]{1,0:T(8,128)(2,1)}, u32[]{:S(2)}) copy-start(bf16[1024,512]{1,0:T(8,128)(2,1)} %param.15) | copy-start | bytes 3145732
  191.2 1.3 copy-start.6
  194.8 2.1 copy-start.10
  195.6 1.3 copy-start.4
  199.0 1.4 copy-start.2
  274.7 4.9 copy-start.18
  313.6 1.9 copy-start.15
  313.8 3.2 copy-start.7
  313.9 3.2 copy-start.9
  315.4 2.4 copy-start.5
  316.2 2.5 copy-start.3
Sparse Core Ops, SparseCore 0:
  10.6 84.6 all-gather.5
  98.5 95.9 all-gather.9
  197.0 95.3 all-gather.7
  296.8 218.3 reduce-scatter.1
where the time goes:
time: 524 us; the launch traced here: 522 us
  waiting for transfers between devices  275 us (52%)
  blocking collectives  84.6 us (16%)
  matrix products  53.9 us (10%)
  other arithmetic  39.3 us (7%)
  local copies, waits for them, and re-layouts  32.3 us (6%)
  loops' own time  21.4 us (4%)
  between operations  14.9 us (3%)
    reduce_scatter x1, waiting for transfers between devices, shards(): lax.psum_scatter((weights[:, None, None, None] * start_grad.astype(jnp.fl...  193 us
    all_gather x1, waiting for transfers between devices, shards(): shard_piece = lax.all_gather(cache_states, 'seq', axis=0, tiled=True)  81.1 us
    unnamed x1, blocking collectives  73.2 us
    select_n x31, other arithmetic, combine_states(): jnp.where(later_item[0] > 0, later_item[1], earlier_item[1] + later_item[1])  32.7 us
    another operation x2, loops' own time, prefix(): return lax.fori_loop(0, ahead, one, state)  21.4 us
    dot_general x8, matrix products, leading_dot(): lax.dot_general(left_rows, right_rows, (((0,), (0,)), ((), ())), preferre...  19.3 us
    dynamic_slice x31, local copies, waits for them, and re-layouts, one(): lax.dynamic_index_in_dim(a, source, 0, False)  18.3 us
    dot_general x16, matrix products, pairwise_dot(): lax.dot_general(left_rows, right_rows, (((1,), (1,)), ((), ())), preferre...  13.4 us
  transfers between devices with their start and end apart: 4, of which 2 were waited for; matrix products, arithmetic and copies ran while one was open for 23% of the time, Pallas kernels for 0%

commit v1 on v0

--- a/solution.py
+++ b/solution.py
@@ -70,7 +70,10 @@
     )
     target = cache_owner[block_index]
     zero_state = jnp.zeros((heads_here, DK, DV), jnp.float32)
-    shard_piece = lax.all_gather(cache_states, "seq", axis=0, tiled=True)
+    size = lax.axis_size("seq")
+    parts = jnp.stack([cache_states for _ in range(size)])
+    parts = lax.all_to_all(parts, "seq", split_axis=0, concat_axis=0)
+    shard_piece = jnp.concatenate(parts, axis=0)
     slot_ids = jnp.arange(shard_piece.shape[0])
     weights = (slot_ids == target).astype(jnp.bfloat16)
     owned_state = lax.dot_general(

time: 524 us -> 560 us (1.069)
  waiting for transfers between devices: 275 us -> 298 us
  starting transfers between devices: 0.16 us -> 11.7 us
    all_to_all x0 -> x1, waiting for transfers between devices: none -> 125 us  [shards(): parts = lax.all_to_all(parts, 'seq', split_axis=0, concat_axis=0)]
    all_gather x1 -> x0, waiting for transfers between devices: 81.1 us -> none  [shards(): shard_piece = lax.all_gather(cache_states, 'seq', axis=0, tiled=True)]
    reduce_scatter x1, waiting for transfers between devices: 193 us -> 173 us  [shards(): lax.psum_scatter((weights[:, None, None, None] * start_grad.astype(jnp.fl...]
    all_to_all x0 -> x1, starting transfers between devices: none -> 11.6 us  [shards(): parts = lax.all_to_all(parts, 'seq', split_axis=0, concat_axis=0)]
  transfers between devices with their start and end apart: 4 -> 4, of which waited for: 2 -> 2; matrix products, arithmetic and copies ran while one was open for 23% -> 21% of each run, Pallas kernels for 0% -> 0%
where the time goes in v1:
time: 560 us; the launch traced here: 558 us
  waiting for transfers between devices  298 us (53%)
  blocking collectives  83.9 us (15%)
  matrix products  52.8 us (9%)
  other arithmetic  39.2 us (7%)
  local copies, waits for them, and re-layouts  35.9 us (6%)
  loops' own time  21.4 us (4%)
  between operations  14.9 us (3%)
  starting transfers between devices  11.7 us (2%)
    reduce_scatter x1, waiting for transfers between devices, shards(): lax.psum_scatter((weights[:, None, None, None] * start_grad.astype(jnp.fl...  173 us
    all_to_all x1, waiting for transfers between devices, shards(): parts = lax.all_to_all(parts, 'seq', split_axis=0, concat_axis=0)  125 us
    unnamed x1, blocking collectives  72.5 us
    select_n x31, other arithmetic, combine_states(): jnp.where(later_item[0] > 0, later_item[1], earlier_item[1] + later_item[1])  32.7 us
    another operation x2, loops' own time, prefix(): return lax.fori_loop(0, ahead, one, state)  21.4 us
    dot_general x8, matrix products, leading_dot(): lax.dot_general(left_rows, right_rows, (((0,), (0,)), ((), ())), preferre...  18.3 us
    dynamic_slice x31, local copies, waits for them, and re-layouts, one(): lax.dynamic_index_in_dim(a, source, 0, False)  18.3 us
    dot_general x16, matrix products, pairwise_dot(): lax.dot_general(left_rows, right_rows, (((1,), (1,)), ((), ())), preferre...  13.3 us
  transfers between devices with their start and end apart: 4, of which 2 were waited for; matrix products, arithmetic and copies ran while one was open for 21% of the time, Pallas kernels for 0%

profile of v1, /device:TPU:8, one launch (start us, length us, event | category | flops | bytes accessed | tf_op | source)
XLA Modules:
  0.0 558.0 jit_solution(3068177628957482658)
XLA Ops:
  9.4 2.8 convolution_multiply_fusion.1
  12.2 3.1 stack.2
  15.3 11.6 %all-to-all-start = ((bf16[32,1,4,128,128]{4,3,2,1,0:T(8,128)(2,1)}), bf16[32,1,4,128,128]{4,3,2,1,0:T(8,128)(2,1)}, u32[]{:S(2)}, u32[]{:S(2)}) async-start(bf16[32,1,4,128,128]{4,3,2,1,0:T(8,128)(2,1)} %stack.2), calls=%async_computation | async-start | bytes 8388608 | tf_op jit(solution)/shard_map/all_to_all | solution.py:75
  28.1 125.1 %all-to-all-done = bf16[32,1,4,128,128]{4,3,2,1,0:T(8,128)(2,1)} async-done(((bf16[32,1,4,128,128]{4,3,2,1,0:T(8,128)(2,1)}), bf16[32,1,4,128,128]{4,3,2,1,0:T(8,128)(2,1)}, u32[]{:S(2)}, u32[]{:S(2)}) %all-to-all-start) | async-done | bytes 4194336 | tf_op jit(solution)/shard_map/all_to_all | solution.py:75
  153.2 5.4 fusion
  162.2 72.5 %all-reduce.1 = (f32[32]{0:T(128)S(1)}, f32[512]{0:T(512)S(1)}) all-reduce(f32[32]{0:T(128)S(1)} %dynamic-update-slice, f32[512]{0:T(512)S(1)} %bitcast.124), channel_id=1, replica_groups=mesh['seq'=32,'head'=8] {'seq'}, use_global_device_ids=true, to_apply=%add | all-reduce | flops 544 | bytes 4352
  235.1 11.4 %psum.15 = f32[1024]{0:T(1024)} all-reduce(f32[1024]{0:T(1024)S(1)} %bitcast.123), channel_id=1, replica_groups=mesh['seq'=32,'head'=8] {'head'}, use_global_device_ids=true, to_apply=%region_6.7 | all-reduce | flops 1024 | bytes 8192 | tf_op jit(solution)/shard_map/psum | solution.py:159
  257.5 1.8 select_convert_fusion.7
  259.3 72.0 %while.27 = (s32[]{:T(128)}, f32[4,128,128]{2,1,0:T(8,128)S(1)}, s32[]{:T(128)}, f32[32]{0:T(128)S(1)}, f32[32,4,128,128]{3,2,1,0:T(8,128)}, /*index=5*/s32[]{:T(128)}, s32[]{:T(128)}, s32[]{:T(128)}, s32[]{:T(128)}, f32[1]{0:T(128)}) while((s32[]{:T(128)}, f32[4,128,128]{2,1,0:T(8,128)S(1)}, s32[]{:T(128)}, f32[32]{0:T(128)S(1)}, ...), condition=%wide.region_3.4_spmd, body=%wide.region_2.3_spmd.sunk | while | flops 131079 | bytes 786613 | solution.py:24
  331.4 1.7 fusion.26
  333.1 3.1 multiply_convert_fusion
  336.8 2.2 fusion.78
  339.0 3.1 fusion.6
  342.1 3.0 fusion.5
  345.2 3.0 fusion.4
  348.2 3.0 fusion.3
  351.3 1.5 fusion.14
  358.4 2.3 copy.31
  360.7 1.5 fusion.18
  362.2 1.6 fusion.17
  363.8 1.6 fusion.16
  365.4 1.6 fusion.15
  368.0 2.3 copy.32
  378.5 173.0 %reduce-scatter.2.cloned.1.call-done = bf16[1,4,128,128]{3,2,1,0:T(8,128)(2,1)} async-done(((bf16[32,4,128,128]{3,2,1,0:T(8,128)(2,1)}), bf16[1,4,128,128]{3,2,1,0:T(8,128)(2,1)}) %reduce-scatter.2.cloned.1.call-update) | async-done | bytes 131088 | tf_op jit(solution)/shard_map/reduce_scatter | solution.py:114
  (156 shorter events, 83.8 us)
Async XLA Ops:
  7.2 154.7 %copy-start = (f32[1024]{0:T(1024)S(1)}, f32[1024]{0:T(1024)}, u32[]{:S(2)}) copy-start(f32[1024]{0:T(1024)} %param.20) | copy-start | bytes 12292
  7.2 5.0 copy-start.15
  7.2 252.1 %all-gather.7.cloned.1.call-start = ((), (), s32[]{:S(2)}) async-start(), calls=%async_computation.4 | async-start | bytes 8650752 | tf_op jit(solution)/shard_map/all_gather | solution.py:15
  9.4 2.8 copy-start.11
  15.3 11.7 %copy-start.8 = (bf16[1024,512]{1,0:T(8,128)(2,1)S(1)}, bf16[1024,512]{1,0:T(8,128)(2,1)}, u32[]{:S(2)}) copy-start(bf16[1024,512]{1,0:T(8,128)(2,1)} %param.14) | copy-start | bytes 3145732
  15.3 12.2 %copy-start.17 = (s32[32]{0:T(128)S(1)}, s32[32]{0:T(128)}, u32[]{:S(2)}) copy-start(s32[32]{0:T(128)} %param.19) | copy-start | bytes 388
  15.3 137.9 %all-to-all-start = ((bf16[32,1,4,128,128]{4,3,2,1,0:T(8,128)(2,1)}), bf16[32,1,4,128,128]{4,3,2,1,0:T(8,128)(2,1)}, u32[]{:S(2)}, u32[]{:S(2)}) async-start(bf16[32,1,4,128,128]{4,3,2,1,0:T(8,128)(2,1)} %stack.2), calls=%async_computation | async-start | bytes 8388608 | tf_op jit(solution)/shard_map/all_to_all | solution.py:75
  26.9 132.4 %copy-start.12 = (bf16[1024,512]{1,0:T(8,128)(2,1)S(1)}, bf16[1024,512]{1,0:T(8,128)(2,1)}, u32[]{:S(2)}) copy-start(bf16[1024,512]{1,0:T(8,128)(2,1)} %param.15) | copy-start | bytes 3145732
  26.9 343.3 %all-gather.5.cloned.1.call-start = ((), (), s32[]{:S(2)}) async-start(), calls=%async_computation.3 | async-start | bytes 8650752 | tf_op jit(solution)/shard_map/all_gather | solution.py:15
  153.2 7.3 %copy-start.16 = (bf16[4,128]{1,0:T(4,128)(2,1)S(1)}, bf16[4,128]{1,0:T(4,128)(2,1)}, u32[]{:S(2)}) copy-start(bf16[4,128]{1,0:T(4,128)(2,1)} %param.21) | copy-start | bytes 3076
  153.2 7.3 %copy-start.19 = (u32[256]{0:T(256)S(1)}, u32[256]{0:T(256)}, u32[]{:S(2)}) copy-start(u32[256]{0:T(256)} %constant.87) | copy-start | bytes 3076
  153.2 8.7 %copy-start.1 = (bf16[1024,512]{1,0:T(8,128)(2,1)S(1)}, bf16[1024,512]{1,0:T(8,128)(2,1)}, u32[]{:S(2)}) copy-start(bf16[1024,512]{1,0:T(8,128)(2,1)} %param.16) | copy-start | bytes 3145732
  158.6 0.7 copy-start.13
  160.5 391.0 %reduce-scatter.2.cloned.1.call-start = ((), (), s32[]{:S(2)}) async-start(), calls=%async_computation.2 | async-start | bytes 4325376 | tf_op jit(solution)/shard_map/reduce_scatter | solution.py:114
  162.2 87.1 %copy-start.10 = (bf16[1024,512]{1,0:T(8,128)(2,1)S(1)}, bf16[1024,512]{1,0:T(8,128)(2,1)}, u32[]{:S(2)}) copy-start(bf16[1024,512]{1,0:T(8,128)(2,1)} %param.13) | copy-start | bytes 3145732
  247.9 1.3 copy-start.6
  251.4 1.3 copy-start.4
  254.8 1.4 copy-start.2
  331.4 4.8 copy-start.18
  370.2 1.9 copy-start.14
  370.5 3.2 copy-start.7
  370.5 3.2 copy-start.9
  372.1 2.4 copy-start.5
  372.9 2.5 copy-start.3
Sparse Core Ops, SparseCore 0:
  12.3 157.5 all-gather.6
  172.5 97.2 all-gather.4
  336.3 215.1 reduce-scatter.1
